TPU v7x, 512 devices: a whole 4x8x8 slice. The times are simulated.
512 devices in a mesh: tm: 16 (over x, z_hi, core), coef: 32 (over y, z_lo).
Axes of the slice: x: 4, y: 8, z: 8 (z_hi: 2, z_lo: 4; z = z_hi * 4 + z_lo), core: 2. Of those that a mesh axis runs over, the one named last changes fastest.
Arguments:
- design: float32 [8192, 40960], P('tm', 'coef'), may hold values from -4 to 4
- whitening: float32 [8192, 256], P('tm'), may hold values from -1 to 3, as said below
- solution: float32 [40960, 64], P('coef'), may hold values from -6 to 6
- direction: float32 [40960, 64], P('coef'), may hold values from -6 to 6
- gradient_prev: float32 [40960, 64], P('coef'), may hold values from -25 to 25
- residual: float32 [8192, 64], P('tm'), may hold values from -6 to 6
Outputs:
- new_solution: float32 [40960, 64], P('coef')
- new_residual: float32 [8192, 64], P('tm')
- new_direction: float32 [40960, 64], P('coef')
Inputs may be any that keep to these rules, and one draw needn't show every extreme that they name: `whitening`: the first tap of every row is positive.
All inputs are finite; a program needn't handle non-finite values.
Results may differ from a plain program's by a relative error of at most 0.00008.
Values sent between devices are 32-bit elements; how exact they have to be, the bound alone decides.
No kernel may reach another device: no remote copies, remote signals or barrier semaphores. Data moves between devices by JAX's collectives and lax.ppermute only.
A program may use at most 64 MiB of HBM per device.

v0:
```python
import jax
import jax.numpy as jnp
from jax import lax
from jax.experimental import pallas as pl
from jax.experimental.pallas import tpu as pltpu
from jax.sharding import PartitionSpec as P


BLOCK = 256
NN = (((1,), (0,)), ((), ()))
NT = (((1,), (1,)), ((), ()))
F32, BF16 = jnp.float32, jnp.bfloat16


def split(values):
    high = values.astype(BF16)
    return high, (values - high.astype(F32)).astype(BF16)


def times(left, right, dims):
    high, low = split(left)
    count = left.shape[0]
    first = lax.dot_general(jnp.concatenate([high, low], axis=0), right[0], dims, preferred_element_type=F32)
    return first[:count] + first[count:] + lax.dot_general(high, right[1], dims, preferred_element_type=F32)


def skew(rows):
    return pltpu.roll(rows, 0, 1, stride=1, stride_axis=0)


def as_row(column):
    shape = (column.shape[0], 128)
    pick = lax.broadcasted_iota(jnp.int32, shape, 0) == lax.broadcasted_iota(jnp.int32, shape, 1)
    return jnp.sum(jnp.where(pick, jnp.broadcast_to(column, shape), 0.0), axis=0, keepdims=True)


def row_squares(values):
    total = values[:, :128] * values[:, :128]
    for k in range(128, values.shape[1], 128):
        total = total + values[:, k : k + 128] * values[:, k : k + 128]
    return as_row(jnp.sum(total, axis=1, keepdims=True))


def as_column(row, first, count):
    shape = (count, 128)
    pick = lax.broadcasted_iota(jnp.int32, shape, 1) == lax.broadcasted_iota(jnp.int32, shape, 0) + first
    return jnp.sum(jnp.where(pick, jnp.broadcast_to(row[:1], shape), 0.0), axis=1, keepdims=True)


def collect(rows):
    tile, old = rows[:8], rows[8:9]
    for m in range(1, 32):
        tile = tile + rows[9 * m : 9 * m + 8]
        old = old + rows[9 * m + 8 : 9 * m + 9]
    return tile, jnp.broadcast_to(old, (8, 128))


def chunk(tile, rim):
    return jnp.concatenate([tile, rim] * 32, axis=0)


def band(whitening, rim, residual, design):
    taps = jnp.concatenate([whitening, rim[:BLOCK]], axis=0)
    lag = lax.broadcasted_iota(jnp.int32, (BLOCK, BLOCK), 0)
    lane = lax.broadcasted_iota(jnp.int32, (BLOCK, BLOCK), 1)
    mirror = jnp.where((lag + lane) % BLOCK == 0, 1.0, 0.0).astype(BF16)
    high, low = split(taps)
    least = (taps - high.astype(F32) - low.astype(F32)).astype(BF16)
    count = taps.shape[0]
    turned = lax.dot_general(jnp.concatenate([high, low, least], axis=0), mirror, NN, preferred_element_type=F32)
    turned = turned[:count] + turned[count : 2 * count] + turned[2 * count :]
    same, before = [], []
    for b in range(3):
        full = skew(turned[BLOCK * b : BLOCK * (b + 1)])
        same.append(split(jnp.where(lane <= lag, full, 0.0)))
        before.append(split(jnp.where(lane > lag, full, 0.0)))
    res = [residual[:, :BLOCK], residual[:, BLOCK:], rim[BLOCK:]]
    back = [times(res[b], same[b], NN) + times(res[b + 1], before[b + 1], NN) for b in range(2)]
    bands = [jnp.stack([m[k] for m in kind]) for kind in (same, before) for k in range(2)]
    return *bands, times(jnp.concatenate(back, axis=1), split(design()), NN)


def whiten_and_project(odd, gathered, same_high, same_low, before_high, before_low, back_grad, design):
    def block(halves, row, swap=0):
        return jnp.concatenate(
            [
                jnp.concatenate([gathered[16 * m + row : 16 * m + row + 8] for m in (8 * i + (j ^ swap) for i in halves)], axis=1)
                for j in range(8)
            ],
            axis=0,
        )

    same = [(same_high[b], same_low[b]) for b in range(3)]
    before = [(before_high[b], before_low[b]) for b in range(3)]
    plain = [
        jnp.where(odd, block((2, 3), 8), block((2, 3), 8, 2)),
        block((0, 1), 0),
        block((2, 3), 0),
        jnp.where(odd, block((0, 1), 8, 2), block((0, 1), 8)),
    ]
    pred = [times(plain[b + 1], same[b], NT) + times(plain[b], before[b], NT) for b in range(3)]
    own = jnp.concatenate(pred[:2], axis=1)
    energy = jnp.broadcast_to(row_squares(own), (64, 128))
    spread = [times(pred[b], same[b], NN) + times(pred[b + 1], before[b + 1], NN) for b in range(2)]
    left = jnp.concatenate(spread, axis=1)
    parts = []
    for k in range(back_grad.shape[1] // BLOCK):
        parts.append(times(left, split(design(k)), NN))
    return jnp.concatenate([back_grad, *parts, energy], axis=1), own


def sum_pieces(pieces):
    total = pieces[:8]
    for m in range(1, 8):
        total = total + pieces[8 * m : 8 * m + 8]
    return total


def own_group(place):
    return (lax.shift_right_logical(place[0], 2) * 2 + (place[0] & 1)) * 8


def step_piece(place, mine, other, old):
    total = mine + other
    count = (total.shape[1] - 128) // 2
    alpha = old / total[:, 2 * count :]
    alpha = jnp.where(lax.broadcasted_iota(jnp.int32, alpha.shape, 1) < 64, alpha, 0.0)
    grad = total[:, :count] - as_column(alpha, own_group(place), 8) * total[:, count : 2 * count]
    return grad, alpha, jnp.broadcast_to(row_squares(grad), (32, 128))


def direction_piece(place, norms, grad, old, direction):
    norm = jnp.sum(norms, axis=0, keepdims=True)
    beta = as_column(norm, 0, 8) / as_column(old, own_group(place), 8)
    mine = direction[pl.ds(pl.multiple_of(own_group(place), 8), 8), :]
    return jnp.concatenate([grad + beta * mine] * 8, axis=0)


def update(alpha, solution, direction, residual, predicted):
    step = as_column(alpha, 0, 64)
    return solution + step * direction, residual - step * predicted


def run(function, outs, *args, keep=(), close=(), away=()):
    def kernel(*refs):
        values = [r if k in keep else r[...] for k, r in enumerate(refs[: len(args)])]
        results = function(*values)
        results = results if isinstance(results, tuple) else (results,)
        for ref, value in zip(refs[len(args) :], results, strict=True):
            ref[...] = value

    spaces = [pltpu.SMEM if a.dtype == jnp.int32 else pltpu.VMEM for a in args]
    args = [near(a) if k in close else a for k, a in enumerate(args)]
    outs = [s if isinstance(s, tuple) and isinstance(s[0], tuple) else (s, F32) for s in outs]
    got = pl.pallas_call(
        kernel,
        out_shape=[(pltpu.HBM if k in away else pltpu.VMEM)(s, d) for k, (s, d) in enumerate(outs)],
        in_specs=[pl.BlockSpec(memory_space=s) for s in spaces],
        out_specs=[pl.BlockSpec(memory_space=pltpu.VMEM) for _ in outs],
        compiler_params=pltpu.CompilerParams(vmem_limit_bytes=24 << 20),
    )(*args)
    return got if len(outs) > 1 else got[0]


def near(array):
    return pltpu.with_memory_space_constraint(array, pltpu.VMEM)


def far(array):
    return pltpu.with_memory_space_constraint(array, pltpu.HBM)


LIMIT = pltpu.CompilerParams(vmem_limit_bytes=24 << 20)
HBM, VMEM = pl.BlockSpec(memory_space=pltpu.HBM), pl.BlockSpec(memory_space=pltpu.VMEM)


def predict(direction, design, gradient_prev, whitening, residual):
    def kernel(direction, design, gradient_prev, whitening, residual, rows, rim, dir_v, des_v, old_v, rows_v, sems):
        def copy(source, target, k):
            copies.append(pltpu.make_async_copy(source, target, sems.at[k]))
            copies[-1].start()

        copies = []
        copy(direction, dir_v, 0)
        copy(gradient_prev, old_v, 1)
        for i in range(4):
            copy(design.at[128 * i : 128 * i + 128], des_v.at[128 * i : 128 * i + 128], 2 + i)
        copy(whitening.at[:BLOCK], rim.at[:BLOCK], 6)
        copy(residual.at[:, :BLOCK], rim.at[BLOCK:], 7)
        copies[0].wait()
        left = dir_v[...]
        copies[1].wait()
        old = row_squares(old_v[...])
        for m in range(32):
            rows_v[9 * m + 8 : 9 * m + 9] = old
        for i in range(4):
            copies[2 + i].wait()
            part = times(left, split(des_v[128 * i : 128 * i + 128]), NT)
            for j in range(8):
                first = 9 * (8 * i + j)
                rows_v[first : first + 8] = part[8 * j : 8 * j + 8]
            copy(rows_v.at[72 * i : 72 * i + 72], rows.at[72 * i : 72 * i + 72], 8 + i)
        for k in range(6, 12):
            copies[k].wait()

    return pl.pallas_call(
        kernel,
        out_shape=[
            pltpu.HBM((9 * 32, 128), F32),
            pltpu.VMEM((BLOCK + 64, BLOCK), F32),
        ],
        in_specs=[HBM] * 5,
        out_specs=[HBM, VMEM],
        scratch_shapes=[
            pltpu.VMEM(direction.shape, F32),
            pltpu.VMEM(design.shape, F32),
            pltpu.VMEM(gradient_prev.shape, F32),
            pltpu.VMEM((9 * 32, 128), F32),
            pltpu.SemaphoreType.DMA((12,)),
        ],
        compiler_params=LIMIT,
        name="predict",
    )(*[far(a) for a in (direction, design, gradient_prev, whitening, residual)])


def banded(place, whitening, rim, residual, design):
    def kernel(place, rim, whitening, residual, design, b0, b1, b2, b3, back_grad, tap_v, res_v, des_v, sems):
        copies = [
            pltpu.make_async_copy(source, target, sems.at[k])
            for k, (source, target) in enumerate(((whitening, tap_v), (residual, res_v), (design, des_v)))
        ]
        for copy in copies:
            copy.start()
        for copy in copies[:2]:
            copy.wait()

        def fetched():
            copies[2].wait()
            return des_v[...]

        b0[...], b1[...], b2[...], b3[...], back_grad[...] = band(tap_v[...], rim[...], res_v[...], fetched)

    args = (whitening, residual, design)
    return pl.pallas_call(
        kernel,
        out_shape=[pltpu.VMEM((3, BLOCK, BLOCK), BF16)] * 4 + [pltpu.VMEM((64, design.shape[1]), F32)],
        in_specs=[pl.BlockSpec(memory_space=pltpu.SMEM), VMEM] + [HBM] * 3,
        out_specs=[VMEM] * 5,
        scratch_shapes=[pltpu.VMEM(a.shape, F32) for a in args] + [pltpu.SemaphoreType.DMA((3,))],
        compiler_params=LIMIT,
        name="band",
    )(place, near(rim), *[far(a) for a in args])


def project(place, gathered, bands, back_grad, design):
    count = design.shape[1] // BLOCK

    def kernel(place, gathered, b0, b1, b2, b3, back_grad, design, pieces, predicted, des_v, sems):
        copies = []
        for k in range(count):
            cut = pl.ds(BLOCK * k, BLOCK)
            copies.append(pltpu.make_async_copy(design.at[:, cut], des_v.at[:, cut], sems.at[k]))
            copies[-1].start()

        def fetched(k):
            copies[k].wait()
            return des_v[:, BLOCK * k : BLOCK * (k + 1)]

        pieces[...], predicted[...] = whiten_and_project(
            (place[0] & 1) == 1, gathered[...], b0[...], b1[...], b2[...], b3[...], back_grad[...], fetched
        )

    return pl.pallas_call(
        kernel,
        out_shape=[pltpu.VMEM((64, 2 * design.shape[1] + 128), F32), pltpu.VMEM((64, design.shape[0]), F32)],
        in_specs=[pl.BlockSpec(memory_space=pltpu.SMEM)] + [VMEM] * 6 + [HBM],
        out_specs=[VMEM] * 2,
        scratch_shapes=[pltpu.VMEM(design.shape, F32), pltpu.SemaphoreType.DMA((count,))],
        compiler_params=LIMIT,
        name="whiten_and_project",
    )(place, near(gathered), *[near(b) for b in bands], near(back_grad), far(design))


def exchange(rows, axis, groups=None):
    return lax.all_to_all(rows, axis, 0, 0, axis_index_groups=groups, tiled=True)


def neighbours(blocks_t, blocks_c, step):
    pairs = []
    for t in range(blocks_t):
        for c in range(blocks_c):
            to = t + step(c)
            if 0 <= to < blocks_t:
                pairs.append((t * blocks_c + c, to * blocks_c + (c if t // 2 == to // 2 else c ^ 2)))
    return pairs


def per_device(design, whitening, solution, direction, gradient_prev, residual):
    blocks_t, blocks_c = lax.axis_size("tm"), lax.axis_size("coef")
    coefs = design.shape[1]
    solution, direction, gradient_prev, residual = solution.T, direction.T, gradient_prev.T, residual.T
    groups = [[4 * x + 2 * z + k for x in range(4) for k in range(2)] for z in range(2)]
    t = lax.axis_index("tm").astype(jnp.int32)
    place = t[None]
    rows, rim = predict(direction, design, gradient_prev, whitening, residual)
    rows = exchange(rows.reshape(32, 9 * 128), "coef").reshape(9 * 32, 128)
    rim = lax.ppermute(rim, ("tm", "coef"), neighbours(blocks_t, blocks_c, lambda c: -1))
    *bands, back_grad = banded(place, whitening, rim, residual, design)
    tile, old = run(collect, [(8, 128), (8, 128)], rows, close=(0,))
    rim_tile = lax.ppermute(
        tile, ("tm", "coef"), neighbours(blocks_t, blocks_c, lambda c: 1 if c >= blocks_c // 2 else -1)
    )
    gathered = exchange(run(chunk, [(16 * 32, 128)], tile, rim_tile, close=(0, 1), away=(0,)), "coef")
    pieces, predicted = project(place, gathered, bands, back_grad, design)
    mine = run(sum_pieces, [(8, 2 * coefs + 128)], exchange(pieces, "tm", groups), close=(0,))
    other = lax.ppermute(mine, "tm", [(i, i ^ 2) for i in range(blocks_t)])
    grad, alpha, norms = run(
        step_piece, [(8, coefs), (8, 128), (32, 128)], place, mine, other, old, keep=(0,), close=(1, 2, 3), away=(2,)
    )
    norms = exchange(norms, "coef")
    new_solution, new_residual = run(
        update,
        [solution.shape, residual.shape],
        alpha,
        solution,
        direction,
        residual,
        predicted,
        close=(0, 4),
        away=(0, 1),
    )
    pieces = run(direction_piece, [(64, coefs)], place, norms, grad, old, direction, keep=(0, 4), close=(1, 2, 3))
    return new_solution.T, new_residual.T, exchange(pieces, "tm", groups).T


def solution(mesh):
    return jax.shard_map(
        per_device,
        mesh=mesh,
        in_specs=(
            P("tm", "coef"),
            P("tm", None),
            P("coef", None),
            P("coef", None),
            P("coef", None),
            P("tm", None),
        ),
        out_specs=(P("coef", None), P("tm", None), P("coef", None)),
        check_vma=False,
    )
```

profile of v0, /device:TPU:1, one launch (start us, length us, event | category | flops | bytes accessed | tf_op | source)
XLA Modules:
  0.0 122.8 jit_solution(12308463727939174393)
XLA Ops:
  0.6 3.9 %predict.1 = (f32[288,128]{1,0:T(8,128)}, f32[320,256]{1,0:T(8,128)S(1)}) custom-call(f32[64,1280]{1,0:T(8,128)} %bitcast.21, f32[512,1280]{1,0:T(8,128)} %design.5, f32[64,1280]{1,0:T(8,128)} %bitcast.35, f32[512,256]{1,0:T(8,128)} %whitening.3, f32[64,512]{1,0:T(8,128)} %bitcast.25), custom_call_target="tpu_custom_call" | custom-call | tf_op jit(solution)/shard_map/predict/pallas_call | solution.py:206
  4.6 23.5 %all_to_all.54 = f32[32,1,1152]{2,1,0:T(1,128)S(1)} all-to-all(f32[32,1,1152]{2,1,0:T(1,128)} %bitcast.36), channel_id=1, replica_groups=mesh['tm'=16,'coef'=32] {'coef'}, dimensions={0} | all-to-all | bytes 294912 | tf_op jit(solution)/shard_map/all_to_all | solution.py:285
  28.1 4.2 %collective-permute-start = (f32[8,128]{1,0:T(8,128)S(1)}, f32[8,128]{1,0:T(8,128)S(1)}, u32[]{:S(2)}, u32[]{:S(2)}) collective-permute-start(f32[8,128]{1,0:T(8,128)S(1)} %get-tuple-element.20.refs_0_), channel_id=1, source_target_pairs={{16,48},{17,49},{18,50},{19,51},{20,52},{21,53},{22,54},{23,55},{2... | collective-permute-start | bytes 12296 | tf_op jit(solution)/shard_map/ppermute | solution.py:310
  32.3 5.0 %collective-permute-done.refs_1_ = f32[8,128]{1,0:T(8,128)S(1)} collective-permute-done((f32[8,128]{1,0:T(8,128)S(1)}, f32[8,128]{1,0:T(8,128)S(1)}, u32[]{:S(2)}, u32[]{:S(2)}) %collective-permute-start) | collective-permute-done | bytes 4128 | tf_op jit(solution)/shard_map/ppermute | solution.py:310
  37.4 0.7 shard_map.86
  38.1 4.5 %all-to-all-start.1 = ((f32[32,16,128]{2,1,0:T(8,128)}), f32[32,16,128]{2,1,0:T(8,128)S(1)}, u32[]{:S(2)}, u32[]{:S(2)}) async-start(f32[32,16,128]{2,1,0:T(8,128)} %bitcast.34), calls=%async_computation.1 | async-start | bytes 524288 | tf_op jit(solution)/shard_map/all_to_all | solution.py:285
  42.6 1.9 %collective-permute-start.1 = (f32[320,256]{1,0:T(8,128)S(1)}, f32[320,256]{1,0:T(8,128)S(1)}, u32[]{:S(2)}, u32[]{:S(2)}) collective-permute-start(f32[320,256]{1,0:T(8,128)S(1)} %get-tuple-element.21), channel_id=1, source_target_pairs={{32,0},{33,1},{34,2},{35,3},{36,4},{37,5},{38,6},{39,7},{40,8},{41... | collective-permute-start | bytes 983048 | tf_op jit(solution)/shard_map/ppermute | solution.py:307
  44.5 12.3 %collective-permute-done.1.rim = f32[320,256]{1,0:T(8,128)S(1)} collective-permute-done((f32[320,256]{1,0:T(8,128)S(1)}, f32[320,256]{1,0:T(8,128)S(1)}, u32[]{:S(2)}, u32[]{:S(2)}) %collective-permute-start.1) | collective-permute-done | bytes 327712 | tf_op jit(solution)/shard_map/ppermute | solution.py:307
  56.8 3.1 %band.1 = (bf16[3,256,256]{2,1,0:T(8,128)(2,1)S(1)}, bf16[3,256,256]{2,1,0:T(8,128)(2,1)S(1)}, bf16[3,256,256]{2,1,0:T(8,128)(2,1)S(1)}, bf16[3,256,256]{2,1,0:T(8,128)(2,1)S(1)}, f32[64,1280]{1,0:T(8,128)S(1)}) custom-call(s32[1]{0:T(128)} %bitcast.place.refs_0_, f32[320,256]{1,0:T(8,128)S(1)} %collective-permute-done.1.rim, f32[512,256]{1,0:T(8,128)} %whitening.3, ...), custom_call_target="tpu_custom_call" | custom-call | tf_op jit(solution)/shard_map/band/pallas_call | solution.py:244
  60.0 0.0 all-to-all-done.1
  60.0 0.0 copy-start
  60.0 3.1 %whiten_and_project.1 = (f32[64,2688]{1,0:T(8,128)S(1)}, f32[64,512]{1,0:T(8,128)S(1)}) custom-call(s32[1]{0:T(128)} %bitcast.place.refs_0_, f32[512,128]{1,0:T(8,128)S(1)} %bitcast.28, bf16[3,256,256]{2,1,0:T(8,128)(2,1)S(1)} %get-tuple-element.22.b0, bf16[3,256,256]{2,1,0:T(8,128)(2,1)S(1)} %get-tuple-element.23.b1, ...), custom_call_target="tpu_custom_call" | custom-call | tf_op jit(solution)/shard_map/whiten_and_project/pallas_call | solution.py:273
  63.1 0.0 copy-start.1
  63.1 0.0 copy-start.2
  63.1 15.6 %all_to_all.55 = f32[8,8,2688]{2,1,0:T(8,128)S(1)} all-to-all(f32[8,8,2688]{2,1,0:T(8,128)S(1)} %bitcast.29), channel_id=1, replica_groups={{0,32,128,160,256,288,384,416},{64,96,192,224,320,352,448,480},{1,33,12..., dimensions={0} | all-to-all | bytes 1376256 | tf_op jit(solution)/shard_map/all_to_all | solution.py:285
  78.8 4.9 %collective-permute-start.2 = (f32[8,2688]{1,0:T(8,128)S(1)}, f32[8,2688]{1,0:T(8,128)S(1)}, u32[]{:S(2)}, u32[]{:S(2)}) collective-permute-start(f32[8,2688]{1,0:T(8,128)S(1)} %shard_map.87.refs_1_), channel_id=1, source_target_pairs={{0,64},{32,96},{64,0},{96,32},{128,192},{160,224},{192,128},{224,1... | collective-permute-start | bytes 258056 | tf_op jit(solution)/shard_map/ppermute | solution.py:316
  83.7 4.4 %collective-permute-done.2.refs_2_ = f32[8,2688]{1,0:T(8,128)S(1)} collective-permute-done((f32[8,2688]{1,0:T(8,128)S(1)}, f32[8,2688]{1,0:T(8,128)S(1)}, u32[]{:S(2)}, u32[]{:S(2)}) %collective-permute-start.2) | collective-permute-done | bytes 86048 | tf_op jit(solution)/shard_map/ppermute | solution.py:316
  88.1 0.8 shard_map.88
  88.9 19.6 %all_to_all.56 = f32[32,1,128]{2,1,0:T(1,128)S(1)} all-to-all(f32[32,1,128]{2,1,0:T(1,128)} %bitcast.37), channel_id=1, replica_groups=mesh['tm'=16,'coef'=32] {'coef'}, dimensions={0} | all-to-all | bytes 32768 | tf_op jit(solution)/shard_map/all_to_all | solution.py:285
  108.5 0.0 copy-done
  108.5 0.8 shard_map.90
  109.3 5.6 %all-to-all-start.4 = ((f32[8,8,1280]{2,1,0:T(8,128)}), f32[8,8,1280]{2,1,0:T(8,128)S(1)}, u32[]{:S(2)}, u32[]{:S(2)}) async-start(f32[8,8,1280]{2,1,0:T(8,128)} %bitcast.16), calls=%async_computation.4 | async-start | bytes 655360 | tf_op jit(solution)/shard_map/all_to_all | solution.py:285
  115.0 0.0 copy-done.1
  115.0 0.0 copy-done.2
  115.0 0.9 shard_map.89
  115.9 6.2 %all-to-all-done.4 = f32[8,8,1280]{2,1,0:T(8,128)S(1)} async-done(((f32[8,8,1280]{2,1,0:T(8,128)}), f32[8,8,1280]{2,1,0:T(8,128)S(1)}, u32[]{:S(2)}, u32[]{:S(2)}) %all-to-all-start.4) | async-done | bytes 327712 | tf_op jit(solution)/shard_map/all_to_all | solution.py:285
  122.1 0.7 copy.12
  (2 shorter events, 0.1 us)
Async XLA Ops:
  28.1 9.2 %collective-permute-start = (f32[8,128]{1,0:T(8,128)S(1)}, f32[8,128]{1,0:T(8,128)S(1)}, u32[]{:S(2)}, u32[]{:S(2)}) collective-permute-start(f32[8,128]{1,0:T(8,128)S(1)} %get-tuple-element.20.refs_0_), channel_id=1, source_target_pairs={{16,48},{17,49},{18,50},{19,51},{20,52},{21,53},{22,54},{23,55},{2... | collective-permute-start | bytes 12296 | tf_op jit(solution)/shard_map/ppermute | solution.py:310
  38.1 21.9 %all-to-all-start.1 = ((f32[32,16,128]{2,1,0:T(8,128)}), f32[32,16,128]{2,1,0:T(8,128)S(1)}, u32[]{:S(2)}, u32[]{:S(2)}) async-start(f32[32,16,128]{2,1,0:T(8,128)} %bitcast.34), calls=%async_computation.1 | async-start | bytes 524288 | tf_op jit(solution)/shard_map/all_to_all | solution.py:285
  42.6 14.2 %collective-permute-start.1 = (f32[320,256]{1,0:T(8,128)S(1)}, f32[320,256]{1,0:T(8,128)S(1)}, u32[]{:S(2)}, u32[]{:S(2)}) collective-permute-start(f32[320,256]{1,0:T(8,128)S(1)} %get-tuple-element.21), channel_id=1, source_target_pairs={{32,0},{33,1},{34,2},{35,3},{36,4},{37,5},{38,6},{39,7},{40,8},{41... | collective-permute-start | bytes 983048 | tf_op jit(solution)/shard_map/ppermute | solution.py:307
  60.0 48.5 %copy-start = (f32[1280,64]{0,1:T(8,128)S(1)}, f32[1280,64]{0,1:T(8,128)}, u32[]{:S(2)}) copy-start(f32[1280,64]{0,1:T(8,128)} %param.9) | copy-start | bytes 983044
  63.1 51.9 %copy-start.1 = (f32[512,64]{0,1:T(8,128)S(1)}, f32[512,64]{0,1:T(8,128)}, u32[]{:S(2)}) copy-start(f32[512,64]{0,1:T(8,128)} %param.11) | copy-start | bytes 393220
  63.1 51.9 %copy-start.2 = (f32[1280,64]{0,1:T(8,128)S(1)}, f32[1280,64]{0,1:T(8,128)}, u32[]{:S(2)}) copy-start(f32[1280,64]{0,1:T(8,128)} %param.8) | copy-start | bytes 983044
  78.8 9.2 %collective-permute-start.2 = (f32[8,2688]{1,0:T(8,128)S(1)}, f32[8,2688]{1,0:T(8,128)S(1)}, u32[]{:S(2)}, u32[]{:S(2)}) collective-permute-start(f32[8,2688]{1,0:T(8,128)S(1)} %shard_map.87.refs_1_), channel_id=1, source_target_pairs={{0,64},{32,96},{64,0},{96,32},{128,192},{160,224},{192,128},{224,1... | collective-permute-start | bytes 258056 | tf_op jit(solution)/shard_map/ppermute | solution.py:316
  109.3 12.8 %all-to-all-start.4 = ((f32[8,8,1280]{2,1,0:T(8,128)}), f32[8,8,1280]{2,1,0:T(8,128)S(1)}, u32[]{:S(2)}, u32[]{:S(2)}) async-start(f32[8,8,1280]{2,1,0:T(8,128)} %bitcast.16), calls=%async_computation.4 | async-start | bytes 655360 | tf_op jit(solution)/shard_map/all_to_all | solution.py:285
where the time goes:
time: 123 us
  blocking collectives  58.8 us (48%)
  waiting for transfers between devices  27.9 us (23%)
  starting transfers between devices  21.1 us (17%)
  Pallas kernels  13.5 us (11%)
    all_to_all x3, blocking collectives, exchange(): lax.all_to_all(rows, axis, 0, 0, axis_index_groups=groups, tiled=True)  58.8 us
    ppermute x1, waiting for transfers between devices, per_device(): lax.ppermute(rim, ('tm', 'coef'), neighbours(blocks_t, blocks_c, lambda c...  12.3 us
    all_to_all x2, starting transfers between devices, exchange(): lax.all_to_all(rows, axis, 0, 0, axis_index_groups=groups, tiled=True)  10.1 us
    all_to_all x2, waiting for transfers between devices, exchange(): lax.all_to_all(rows, axis, 0, 0, axis_index_groups=groups, tiled=True)  6.22 us
    ppermute x1, waiting for transfers between devices, per_device(): lax.ppermute(tile, ('tm', 'coef'), neighbours(blocks_t, blocks_c, lambda...  5.04 us
    ppermute x1, starting transfers between devices, per_device(): other = lax.ppermute(mine, 'tm', [(i, i ^ 2) for i in range(blocks_t)])  4.86 us
    ppermute x1, waiting for transfers between devices, per_device(): other = lax.ppermute(mine, 'tm', [(i, i ^ 2) for i in range(blocks_t)])  4.37 us
    ppermute x1, starting transfers between devices, per_device(): lax.ppermute(tile, ('tm', 'coef'), neighbours(blocks_t, blocks_c, lambda...  4.18 us
  transfers between devices with their start and end apart: 5, of which 4 were waited for; matrix products, arithmetic and copies ran while one was open for 0% of the time, Pallas kernels for 3%

commit v1 on v0

--- a/solution.py
+++ b/solution.py
@@ -80,7 +80,7 @@
     return *bands, times(jnp.concatenate(back, axis=1), split(design()), NN)
 
 
-def whiten_and_project(odd, gathered, same_high, same_low, before_high, before_low, back_grad, design):
+def whiten_and_project(odd, gathered, same_high, same_low, before_high, before_low, keep, got, design):
     def block(halves, row, swap=0):
         return jnp.concatenate(
             [
@@ -104,9 +104,9 @@
     spread = [times(pred[b], same[b], NN) + times(pred[b + 1], before[b + 1], NN) for b in range(2)]
     left = jnp.concatenate(spread, axis=1)
     parts = []
-    for k in range(back_grad.shape[1] // BLOCK):
+    for k in range(2 * keep.shape[1] // BLOCK):
         parts.append(times(left, split(design(k)), NN))
-    return jnp.concatenate([back_grad, *parts, energy], axis=1), own
+    return jnp.concatenate([keep + got, *parts, energy], axis=1), own
 
 
 def sum_pieces(pieces):
@@ -116,16 +116,28 @@
     return total
 
 
+def upper(place):
+    return (place[0] & 2) == 2
+
+
+def halves_of(values, swap):
+    half = values.shape[1] // 2
+    first, second = values[:, :half], values[:, half:]
+    return jnp.where(swap, second, first), jnp.where(swap, first, second)
+
+
 def own_group(place):
     return (lax.shift_right_logical(place[0], 2) * 2 + (place[0] & 1)) * 8
 
 
 def step_piece(place, mine, other, old):
-    total = mine + other
-    count = (total.shape[1] - 128) // 2
-    alpha = old / total[:, 2 * count :]
+    half = (mine.shape[1] - 128) // 3
+    back = jnp.concatenate([mine[:, :half], other[:, :half]], axis=1)
+    back = jnp.concatenate(halves_of(back, upper(place)), axis=1)
+    total = mine[:, half:] + other[:, half:]
+    alpha = old / total[:, 2 * half :]
     alpha = jnp.where(lax.broadcasted_iota(jnp.int32, alpha.shape, 1) < 64, alpha, 0.0)
-    grad = total[:, :count] - as_column(alpha, own_group(place), 8) * total[:, count : 2 * count]
+    grad = back - as_column(alpha, own_group(place), 8) * total[:, : 2 * half]
     return grad, alpha, jnp.broadcast_to(row_squares(grad), (32, 128))
 
 
@@ -224,7 +236,7 @@
 
 
 def banded(place, whitening, rim, residual, design):
-    def kernel(place, rim, whitening, residual, design, b0, b1, b2, b3, back_grad, tap_v, res_v, des_v, sems):
+    def kernel(place, rim, whitening, residual, design, b0, b1, b2, b3, keep, send, tap_v, res_v, des_v, sems):
         copies = [
             pltpu.make_async_copy(source, target, sems.at[k])
             for k, (source, target) in enumerate(((whitening, tap_v), (residual, res_v), (design, des_v)))
@@ -238,24 +250,25 @@
             copies[2].wait()
             return des_v[...]
 
-        b0[...], b1[...], b2[...], b3[...], back_grad[...] = band(tap_v[...], rim[...], res_v[...], fetched)
+        b0[...], b1[...], b2[...], b3[...], back = band(tap_v[...], rim[...], res_v[...], fetched)
+        keep[...], send[...] = halves_of(back, upper(place))
 
     args = (whitening, residual, design)
     return pl.pallas_call(
         kernel,
-        out_shape=[pltpu.VMEM((3, BLOCK, BLOCK), BF16)] * 4 + [pltpu.VMEM((64, design.shape[1]), F32)],
+        out_shape=[pltpu.VMEM((3, BLOCK, BLOCK), BF16)] * 4 + [pltpu.VMEM((64, design.shape[1] // 2), F32)] * 2,
         in_specs=[pl.BlockSpec(memory_space=pltpu.SMEM), VMEM] + [HBM] * 3,
-        out_specs=[VMEM] * 5,
+        out_specs=[VMEM] * 6,
         scratch_shapes=[pltpu.VMEM(a.shape, F32) for a in args] + [pltpu.SemaphoreType.DMA((3,))],
         compiler_params=LIMIT,
         name="band",
     )(place, near(rim), *[far(a) for a in args])
 
 
-def project(place, gathered, bands, back_grad, design):
+def project(place, gathered, bands, keep, got, design):
     count = design.shape[1] // BLOCK
 
-    def kernel(place, gathered, b0, b1, b2, b3, back_grad, design, pieces, predicted, des_v, sems):
+    def kernel(place, gathered, b0, b1, b2, b3, keep, got, design, pieces, predicted, des_v, sems):
         copies = []
         for k in range(count):
             cut = pl.ds(BLOCK * k, BLOCK)
@@ -267,18 +280,18 @@
             return des_v[:, BLOCK * k : BLOCK * (k + 1)]
 
         pieces[...], predicted[...] = whiten_and_project(
-            (place[0] & 1) == 1, gathered[...], b0[...], b1[...], b2[...], b3[...], back_grad[...], fetched
+            (place[0] & 1) == 1, gathered[...], b0[...], b1[...], b2[...], b3[...], keep[...], got[...], fetched
         )
 
     return pl.pallas_call(
         kernel,
-        out_shape=[pltpu.VMEM((64, 2 * design.shape[1] + 128), F32), pltpu.VMEM((64, design.shape[0]), F32)],
-        in_specs=[pl.BlockSpec(memory_space=pltpu.SMEM)] + [VMEM] * 6 + [HBM],
+        out_shape=[pltpu.VMEM((64, design.shape[1] // 2 * 3 + 128), F32), pltpu.VMEM((64, design.shape[0]), F32)],
+        in_specs=[pl.BlockSpec(memory_space=pltpu.SMEM)] + [VMEM] * 7 + [HBM],
         out_specs=[VMEM] * 2,
         scratch_shapes=[pltpu.VMEM(design.shape, F32), pltpu.SemaphoreType.DMA((count,))],
         compiler_params=LIMIT,
         name="whiten_and_project",
-    )(place, near(gathered), *[near(b) for b in bands], near(back_grad), far(design))
+    )(place, near(gathered), *[near(b) for b in bands], near(keep), near(got), far(design))
 
 
 def exchange(rows, axis, groups=None):
@@ -305,15 +318,17 @@
     rows, rim = predict(direction, design, gradient_prev, whitening, residual)
     rows = exchange(rows.reshape(32, 9 * 128), "coef").reshape(9 * 32, 128)
     rim = lax.ppermute(rim, ("tm", "coef"), neighbours(blocks_t, blocks_c, lambda c: -1))
-    *bands, back_grad = banded(place, whitening, rim, residual, design)
+    *bands, keep, send = banded(place, whitening, rim, residual, design)
     tile, old = run(collect, [(8, 128), (8, 128)], rows, close=(0,))
     rim_tile = lax.ppermute(
         tile, ("tm", "coef"), neighbours(blocks_t, blocks_c, lambda c: 1 if c >= blocks_c // 2 else -1)
     )
     gathered = exchange(run(chunk, [(16 * 32, 128)], tile, rim_tile, close=(0, 1), away=(0,)), "coef")
-    pieces, predicted = project(place, gathered, bands, back_grad, design)
-    mine = run(sum_pieces, [(8, 2 * coefs + 128)], exchange(pieces, "tm", groups), close=(0,))
-    other = lax.ppermute(mine, "tm", [(i, i ^ 2) for i in range(blocks_t)])
+    across = [(i, i ^ 2) for i in range(blocks_t)]
+    got = lax.ppermute(send, "tm", across)
+    pieces, predicted = project(place, gathered, bands, keep, got, design)
+    mine = run(sum_pieces, [(8, coefs // 2 * 3 + 128)], exchange(pieces, "tm", groups), close=(0,))
+    other = lax.ppermute(mine, "tm", across)
     grad, alpha, norms = run(
         step_piece, [(8, coefs), (8, 128), (32, 128)], place, mine, other, old, keep=(0,), close=(1, 2, 3), away=(2,)
     )

time: 123 us -> 135 us (1.098)
  waiting for transfers between devices: 27.9 us -> 37.3 us
  starting transfers between devices: 21.1 us -> 24.4 us
  blocking collectives: 58.8 us -> 57.4 us
    ppermute x1 -> x2, waiting for transfers between devices: 4.37 us -> 13.7 us  [the longest x1 6.99 us: per_device(): other = lax.ppermute(mine, 'tm', across)]
    ppermute x1 -> x2, starting transfers between devices: 4.86 us -> 6.92 us  [the longest x1 5 us: per_device(): got = lax.ppermute(send, 'tm', across)]
    all_to_all x3, blocking collectives: 58.8 us -> 57.4 us  [exchange(): lax.all_to_all(rows, axis, 0, 0, axis_index_groups=groups, tiled=True)]
  transfers between devices with their start and end apart: 5 -> 6, of which waited for: 4 -> 5; matrix products, arithmetic and copies ran while one was open for 0% -> 0% of each run, Pallas kernels for 3% -> 3%
where the time goes in v1:
time: 135 us; the launch traced here: 134 us
  blocking collectives  57.4 us (43%)
  waiting for transfers between devices  37.3 us (28%)
  starting transfers between devices  24.4 us (18%)
  Pallas kernels  13.5 us (10%)
    all_to_all x3, blocking collectives, exchange(): lax.all_to_all(rows, axis, 0, 0, axis_index_groups=groups, tiled=True)  57.4 us
    ppermute x1, waiting for transfers between devices, per_device(): lax.ppermute(rim, ('tm', 'coef'), neighbours(blocks_t, blocks_c, lambda c...  12.3 us
    all_to_all x2, starting transfers between devices, exchange(): lax.all_to_all(rows, axis, 0, 0, axis_index_groups=groups, tiled=True)  11.4 us
    ppermute x1, waiting for transfers between devices, per_device(): other = lax.ppermute(mine, 'tm', across)  6.99 us
    ppermute x1, waiting for transfers between devices, per_device(): got = lax.ppermute(send, 'tm', across)  6.72 us
    all_to_all x2, waiting for transfers between devices, exchange(): lax.all_to_all(rows, axis, 0, 0, axis_index_groups=groups, tiled=True)  6.22 us
    ppermute x1, waiting for transfers between devices, per_device(): lax.ppermute(tile, ('tm', 'coef'), neighbours(blocks_t, blocks_c, lambda...  5.04 us
    ppermute x1, starting transfers between devices, per_device(): got = lax.ppermute(send, 'tm', across)  5 us
  transfers between devices with their start and end apart: 6, of which 5 were waited for; matrix products, arithmetic and copies ran while one was open for 0% of the time, Pallas kernels for 3%

profile of v1, /device:TPU:1, one launch (start us, length us, event | category | flops | bytes accessed | tf_op | source)
XLA Modules:
  0.0 134.1 jit_solution(6515541757409793956)
XLA Ops:
  0.6 3.9 %predict.1 = (f32[288,128]{1,0:T(8,128)}, f32[320,256]{1,0:T(8,128)S(1)}) custom-call(f32[64,1280]{1,0:T(8,128)} %bitcast.21, f32[512,1280]{1,0:T(8,128)} %design.5, f32[64,1280]{1,0:T(8,128)} %bitcast.35, f32[512,256]{1,0:T(8,128)} %whitening.3, f32[64,512]{1,0:T(8,128)} %bitcast.25), custom_call_target="tpu_custom_call" | custom-call | tf_op jit(solution)/shard_map/predict/pallas_call | solution.py:218
  4.6 23.5 %all_to_all.54 = f32[32,1,1152]{2,1,0:T(1,128)S(1)} all-to-all(f32[32,1,1152]{2,1,0:T(1,128)} %bitcast.36), channel_id=1, replica_groups=mesh['tm'=16,'coef'=32] {'coef'}, dimensions={0} | all-to-all | bytes 294912 | tf_op jit(solution)/shard_map/all_to_all | solution.py:298
  28.1 4.2 %collective-permute-start = (f32[8,128]{1,0:T(8,128)S(1)}, f32[8,128]{1,0:T(8,128)S(1)}, u32[]{:S(2)}, u32[]{:S(2)}) collective-permute-start(f32[8,128]{1,0:T(8,128)S(1)} %get-tuple-element.21.refs_0_), channel_id=1, source_target_pairs={{16,48},{17,49},{18,50},{19,51},{20,52},{21,53},{22,54},{23,55},{2... | collective-permute-start | bytes 12296 | tf_op jit(solution)/shard_map/ppermute | solution.py:323
  32.3 5.0 %collective-permute-done.refs_1_ = f32[8,128]{1,0:T(8,128)S(1)} collective-permute-done((f32[8,128]{1,0:T(8,128)S(1)}, f32[8,128]{1,0:T(8,128)S(1)}, u32[]{:S(2)}, u32[]{:S(2)}) %collective-permute-start) | collective-permute-done | bytes 4128 | tf_op jit(solution)/shard_map/ppermute | solution.py:323
  37.4 0.7 shard_map.86
  38.1 4.5 %all-to-all-start.1 = ((f32[32,16,128]{2,1,0:T(8,128)}), f32[32,16,128]{2,1,0:T(8,128)S(1)}, u32[]{:S(2)}, u32[]{:S(2)}) async-start(f32[32,16,128]{2,1,0:T(8,128)} %bitcast.34), calls=%async_computation.1 | async-start | bytes 524288 | tf_op jit(solution)/shard_map/all_to_all | solution.py:298
  42.6 1.9 %collective-permute-start.1 = (f32[320,256]{1,0:T(8,128)S(1)}, f32[320,256]{1,0:T(8,128)S(1)}, u32[]{:S(2)}, u32[]{:S(2)}) collective-permute-start(f32[320,256]{1,0:T(8,128)S(1)} %get-tuple-element.22), channel_id=1, source_target_pairs={{32,0},{33,1},{34,2},{35,3},{36,4},{37,5},{38,6},{39,7},{40,8},{41... | collective-permute-start | bytes 983048 | tf_op jit(solution)/shard_map/ppermute | solution.py:320
  44.5 12.3 %collective-permute-done.1.rim = f32[320,256]{1,0:T(8,128)S(1)} collective-permute-done((f32[320,256]{1,0:T(8,128)S(1)}, f32[320,256]{1,0:T(8,128)S(1)}, u32[]{:S(2)}, u32[]{:S(2)}) %collective-permute-start.1) | collective-permute-done | bytes 327712 | tf_op jit(solution)/shard_map/ppermute | solution.py:320
  56.8 3.1 %band.1 = (bf16[3,256,256]{2,1,0:T(8,128)(2,1)S(1)}, bf16[3,256,256]{2,1,0:T(8,128)(2,1)S(1)}, bf16[3,256,256]{2,1,0:T(8,128)(2,1)S(1)}, bf16[3,256,256]{2,1,0:T...) custom-call(s32[1]{0:T(128)} %bitcast.place.refs_0_, f32[320,256]{1,0:T(8,128)S(1)} %collective-permute-done.1.rim, ...), custom_call_target="tpu_custom_call" | custom-call | tf_op jit(solution)/shard_map/band/pallas_call | solution.py:257
  60.0 5.0 %collective-permute-start.2 = (f32[64,640]{1,0:T(8,128)S(1)}, f32[64,640]{1,0:T(8,128)S(1)}, u32[]{:S(2)}, u32[]{:S(2)}) collective-permute-start(f32[64,640]{1,0:T(8,128)S(1)} %get-tuple-element.28), channel_id=1, source_target_pairs={{0,64},{32,96},{64,0},{96,32},{128,192},{160,224},{192,128},{224,1... | collective-permute-start | bytes 491528 | tf_op jit(solution)/shard_map/ppermute | solution.py:328
  65.0 6.7 %collective-permute-done.2.got = f32[64,640]{1,0:T(8,128)S(1)} collective-permute-done((f32[64,640]{1,0:T(8,128)S(1)}, f32[64,640]{1,0:T(8,128)S(1)}, u32[]{:S(2)}, u32[]{:S(2)}) %collective-permute-start.2) | collective-permute-done | bytes 163872 | tf_op jit(solution)/shard_map/ppermute | solution.py:328
  71.7 0.0 all-to-all-done.1
  71.7 0.0 copy-start
  71.7 3.1 %whiten_and_project.1 = (f32[64,2048]{1,0:T(8,128)S(1)}, f32[64,512]{1,0:T(8,128)S(1)}) custom-call(s32[1]{0:T(128)} %bitcast.place.refs_0_, f32[512,128]{1,0:T(8,128)S(1)} %bitcast.28, bf16[3,256,256]{2,1,0:T(8,128)(2,1)S(1)} %get-tuple-element.23.b0, bf16[3,256,256]{2,1,0:T(8,128)(2,1)S(1)} %get-tuple-element.24.b1, ...), custom_call_target="tpu_custom_call" | custom-call | tf_op jit(solution)/shard_map/whiten_and_project/pallas_call | solution.py:286
  74.8 0.0 copy-start.1
  74.8 0.0 copy-start.2
  74.8 16.7 %all_to_all.55 = f32[8,8,2048]{2,1,0:T(8,128)S(1)} all-to-all(f32[8,8,2048]{2,1,0:T(8,128)S(1)} %bitcast.30), channel_id=1, replica_groups={{0,32,128,160,256,288,384,416},{64,96,192,224,320,352,448,480},{1,33,12..., dimensions={0} | all-to-all | bytes 1048576 | tf_op jit(solution)/shard_map/all_to_all | solution.py:298
  91.5 1.9 %collective-permute-start.3 = (f32[8,2048]{1,0:T(8,128)S(1)}, f32[8,2048]{1,0:T(8,128)S(1)}, u32[]{:S(2)}, u32[]{:S(2)}) collective-permute-start(f32[8,2048]{1,0:T(8,128)S(1)} %shard_map.87.refs_1_), channel_id=1, source_target_pairs={{0,64},{32,96},{64,0},{96,32},{128,192},{160,224},{192,128},{224,1... | collective-permute-start | bytes 196616 | tf_op jit(solution)/shard_map/ppermute | solution.py:331
  93.5 7.0 %collective-permute-done.3.refs_2_ = f32[8,2048]{1,0:T(8,128)S(1)} collective-permute-done((f32[8,2048]{1,0:T(8,128)S(1)}, f32[8,2048]{1,0:T(8,128)S(1)}, u32[]{:S(2)}, u32[]{:S(2)}) %collective-permute-start.3) | collective-permute-done | bytes 65568 | tf_op jit(solution)/shard_map/ppermute | solution.py:331
  100.5 0.8 shard_map.88
  101.2 17.2 %all_to_all.56 = f32[32,1,128]{2,1,0:T(1,128)S(1)} all-to-all(f32[32,1,128]{2,1,0:T(1,128)} %bitcast.37), channel_id=1, replica_groups=mesh['tm'=16,'coef'=32] {'coef'}, dimensions={0} | all-to-all | bytes 32768 | tf_op jit(solution)/shard_map/all_to_all | solution.py:298
  118.5 0.0 copy-done
  118.5 0.8 shard_map.90
  119.3 6.9 %all-to-all-start.4 = ((f32[8,8,1280]{2,1,0:T(8,128)}), f32[8,8,1280]{2,1,0:T(8,128)S(1)}, u32[]{:S(2)}, u32[]{:S(2)}) async-start(f32[8,8,1280]{2,1,0:T(8,128)} %bitcast.16), calls=%async_computation.4 | async-start | bytes 655360 | tf_op jit(solution)/shard_map/all_to_all | solution.py:298
  126.2 0.0 copy-done.1
  126.3 0.0 copy-done.2
  126.3 0.9 shard_map.89
  127.1 6.2 %all-to-all-done.4 = f32[8,8,1280]{2,1,0:T(8,128)S(1)} async-done(((f32[8,8,1280]{2,1,0:T(8,128)}), f32[8,8,1280]{2,1,0:T(8,128)S(1)}, u32[]{:S(2)}, u32[]{:S(2)}) %all-to-all-start.4) | async-done | bytes 327712 | tf_op jit(solution)/shard_map/all_to_all | solution.py:298
  133.4 0.7 copy.12
  (2 shorter events, 0.1 us)
Async XLA Ops:
  28.1 9.2 %collective-permute-start = (f32[8,128]{1,0:T(8,128)S(1)}, f32[8,128]{1,0:T(8,128)S(1)}, u32[]{:S(2)}, u32[]{:S(2)}) collective-permute-start(f32[8,128]{1,0:T(8,128)S(1)} %get-tuple-element.21.refs_0_), channel_id=1, source_target_pairs={{16,48},{17,49},{18,50},{19,51},{20,52},{21,53},{22,54},{23,55},{2... | collective-permute-start | bytes 12296 | tf_op jit(solution)/shard_map/ppermute | solution.py:323
  38.1 33.6 %all-to-all-start.1 = ((f32[32,16,128]{2,1,0:T(8,128)}), f32[32,16,128]{2,1,0:T(8,128)S(1)}, u32[]{:S(2)}, u32[]{:S(2)}) async-start(f32[32,16,128]{2,1,0:T(8,128)} %bitcast.34), calls=%async_computation.1 | async-start | bytes 524288 | tf_op jit(solution)/shard_map/all_to_all | solution.py:298
  42.6 14.2 %collective-permute-start.1 = (f32[320,256]{1,0:T(8,128)S(1)}, f32[320,256]{1,0:T(8,128)S(1)}, u32[]{:S(2)}, u32[]{:S(2)}) collective-permute-start(f32[320,256]{1,0:T(8,128)S(1)} %get-tuple-element.22), channel_id=1, source_target_pairs={{32,0},{33,1},{34,2},{35,3},{36,4},{37,5},{38,6},{39,7},{40,8},{41... | collective-permute-start | bytes 983048 | tf_op jit(solution)/shard_map/ppermute | solution.py:320
  60.0 11.7 %collective-permute-start.2 = (f32[64,640]{1,0:T(8,128)S(1)}, f32[64,640]{1,0:T(8,128)S(1)}, u32[]{:S(2)}, u32[]{:S(2)}) collective-permute-start(f32[64,640]{1,0:T(8,128)S(1)} %get-tuple-element.28), channel_id=1, source_target_pairs={{0,64},{32,96},{64,0},{96,32},{128,192},{160,224},{192,128},{224,1... | collective-permute-start | bytes 491528 | tf_op jit(solution)/shard_map/ppermute | solution.py:328
  71.7 46.8 %copy-start = (f32[1280,64]{0,1:T(8,128)S(1)}, f32[1280,64]{0,1:T(8,128)}, u32[]{:S(2)}) copy-start(f32[1280,64]{0,1:T(8,128)} %param.9) | copy-start | bytes 983044
  74.8 51.4 %copy-start.1 = (f32[512,64]{0,1:T(8,128)S(1)}, f32[512,64]{0,1:T(8,128)}, u32[]{:S(2)}) copy-start(f32[512,64]{0,1:T(8,128)} %param.11) | copy-start | bytes 393220
  74.8 51.4 %copy-start.2 = (f32[1280,64]{0,1:T(8,128)S(1)}, f32[1280,64]{0,1:T(8,128)}, u32[]{:S(2)}) copy-start(f32[1280,64]{0,1:T(8,128)} %param.8) | copy-start | bytes 983044
  91.5 8.9 %collective-permute-start.3 = (f32[8,2048]{1,0:T(8,128)S(1)}, f32[8,2048]{1,0:T(8,128)S(1)}, u32[]{:S(2)}, u32[]{:S(2)}) collective-permute-start(f32[8,2048]{1,0:T(8,128)S(1)} %shard_map.87.refs_1_), channel_id=1, source_target_pairs={{0,64},{32,96},{64,0},{96,32},{128,192},{160,224},{192,128},{224,1... | collective-permute-start | bytes 196616 | tf_op jit(solution)/shard_map/ppermute | solution.py:331
  119.3 14.1 %all-to-all-start.4 = ((f32[8,8,1280]{2,1,0:T(8,128)}), f32[8,8,1280]{2,1,0:T(8,128)S(1)}, u32[]{:S(2)}, u32[]{:S(2)}) async-start(f32[8,8,1280]{2,1,0:T(8,128)} %bitcast.16), calls=%async_computation.4 | async-start | bytes 655360 | tf_op jit(solution)/shard_map/all_to_all | solution.py:298

commit v2 on v1

--- a/solution.py
+++ b/solution.py
@@ -110,14 +110,17 @@
 
 
 def sum_pieces(pieces):
-    total = pieces[:8]
+    half = (pieces.shape[1] - 128) // 3
+    part = [pieces[8 * m : 8 * m + 8] for m in range(8)]
+    back = [part[k][:, :half] + part[k + 2][:, :half] + part[k + 4][:, :half] + part[k + 6][:, :half] for k in range(2)]
+    total = part[0][:, half:]
     for m in range(1, 8):
-        total = total + pieces[8 * m : 8 * m + 8]
-    return total
+        total = total + part[m][:, half:]
+    return jnp.concatenate([*back, total], axis=1)
 
 
 def upper(place):
-    return (place[0] & 2) == 2
+    return (place[0] & 1) == 1
 
 
 def halves_of(values, swap):
@@ -131,13 +134,11 @@
 
 
 def step_piece(place, mine, other, old):
-    half = (mine.shape[1] - 128) // 3
-    back = jnp.concatenate([mine[:, :half], other[:, :half]], axis=1)
-    back = jnp.concatenate(halves_of(back, upper(place)), axis=1)
-    total = mine[:, half:] + other[:, half:]
-    alpha = old / total[:, 2 * half :]
+    total = mine + other
+    count = (total.shape[1] - 128) // 2
+    alpha = old / total[:, 2 * count :]
     alpha = jnp.where(lax.broadcasted_iota(jnp.int32, alpha.shape, 1) < 64, alpha, 0.0)
-    grad = back - as_column(alpha, own_group(place), 8) * total[:, : 2 * half]
+    grad = total[:, :count] - as_column(alpha, own_group(place), 8) * total[:, count : 2 * count]
     return grad, alpha, jnp.broadcast_to(row_squares(grad), (32, 128))
 
 
@@ -324,11 +325,10 @@
         tile, ("tm", "coef"), neighbours(blocks_t, blocks_c, lambda c: 1 if c >= blocks_c // 2 else -1)
     )
     gathered = exchange(run(chunk, [(16 * 32, 128)], tile, rim_tile, close=(0, 1), away=(0,)), "coef")
-    across = [(i, i ^ 2) for i in range(blocks_t)]
-    got = lax.ppermute(send, "tm", across)
+    got = lax.ppermute(send, "tm", [(i, i ^ 1) for i in range(blocks_t)])
     pieces, predicted = project(place, gathered, bands, keep, got, design)
-    mine = run(sum_pieces, [(8, coefs // 2 * 3 + 128)], exchange(pieces, "tm", groups), close=(0,))
-    other = lax.ppermute(mine, "tm", across)
+    mine = run(sum_pieces, [(8, 2 * coefs + 128)], exchange(pieces, "tm", groups), close=(0,))
+    other = lax.ppermute(mine, "tm", [(i, i ^ 2) for i in range(blocks_t)])
     grad, alpha, norms = run(
         step_piece, [(8, coefs), (8, 128), (32, 128)], place, mine, other, old, keep=(0,), close=(1, 2, 3), away=(2,)
     )

time: 135 us -> 125 us (0.926)
  waiting for transfers between devices: 37.3 us -> 29.3 us
    ppermute x2, waiting for transfers between devices: 13.7 us -> 5.71 us  [the longest x1 4.35 us: per_device(): other = lax.ppermute(mine, 'tm', [(i, i ^ 2) for i in range(blocks_t)])]
where the time goes in v2:
time: 125 us; the launch traced here: 124 us
  blocking collectives  56.9 us (46%)
  waiting for transfers between devices  29.3 us (23%)
  starting transfers between devices  23.1 us (18%)
  Pallas kernels  13.5 us (11%)
    all_to_all x3, blocking collectives, exchange(): lax.all_to_all(rows, axis, 0, 0, axis_index_groups=groups, tiled=True)  56.9 us
    ppermute x1, waiting for transfers between devices, per_device(): lax.ppermute(rim, ('tm', 'coef'), neighbours(blocks_t, blocks_c, lambda c...  12.3 us
    all_to_all x2, starting transfers between devices, exchange(): lax.all_to_all(rows, axis, 0, 0, axis_index_groups=groups, tiled=True)  10.2 us
    all_to_all x2, waiting for transfers between devices, exchange(): lax.all_to_all(rows, axis, 0, 0, axis_index_groups=groups, tiled=True)  6.22 us
    ppermute x1, waiting for transfers between devices, per_device(): lax.ppermute(tile, ('tm', 'coef'), neighbours(blocks_t, blocks_c, lambda...  5.04 us
    ppermute x1, starting transfers between devices, per_device(): other = lax.ppermute(mine, 'tm', [(i, i ^ 2) for i in range(blocks_t)])  4.88 us
    ppermute x1, waiting for transfers between devices, per_device(): other = lax.ppermute(mine, 'tm', [(i, i ^ 2) for i in range(blocks_t)])  4.35 us
    ppermute x1, starting transfers between devices, per_device(): lax.ppermute(tile, ('tm', 'coef'), neighbours(blocks_t, blocks_c, lambda...  4.18 us
  transfers between devices with their start and end apart: 6, of which 5 were waited for; matrix products, arithmetic and copies ran while one was open for 0% of the time, Pallas kernels for 3%

profile of v2, /device:TPU:1, one launch (start us, length us, event | category | flops | bytes accessed | tf_op | source)
XLA Modules:
  0.0 124.2 jit_solution(17522764538775587714)
XLA Ops:
  0.6 3.9 %predict.1 = (f32[288,128]{1,0:T(8,128)}, f32[320,256]{1,0:T(8,128)S(1)}) custom-call(f32[64,1280]{1,0:T(8,128)} %bitcast.21, f32[512,1280]{1,0:T(8,128)} %design.5, f32[64,1280]{1,0:T(8,128)} %bitcast.35, f32[512,256]{1,0:T(8,128)} %whitening.3, f32[64,512]{1,0:T(8,128)} %bitcast.25), custom_call_target="tpu_custom_call" | custom-call | tf_op jit(solution)/shard_map/predict/pallas_call | solution.py:219
  4.6 23.5 %all_to_all.54 = f32[32,1,1152]{2,1,0:T(1,128)S(1)} all-to-all(f32[32,1,1152]{2,1,0:T(1,128)} %bitcast.36), channel_id=1, replica_groups=mesh['tm'=16,'coef'=32] {'coef'}, dimensions={0} | all-to-all | bytes 294912 | tf_op jit(solution)/shard_map/all_to_all | solution.py:299
  28.1 4.2 %collective-permute-start = (f32[8,128]{1,0:T(8,128)S(1)}, f32[8,128]{1,0:T(8,128)S(1)}, u32[]{:S(2)}, u32[]{:S(2)}) collective-permute-start(f32[8,128]{1,0:T(8,128)S(1)} %get-tuple-element.21.refs_0_), channel_id=1, source_target_pairs={{16,48},{17,49},{18,50},{19,51},{20,52},{21,53},{22,54},{23,55},{2... | collective-permute-start | bytes 12296 | tf_op jit(solution)/shard_map/ppermute | solution.py:324
  32.3 5.0 %collective-permute-done.refs_1_ = f32[8,128]{1,0:T(8,128)S(1)} collective-permute-done((f32[8,128]{1,0:T(8,128)S(1)}, f32[8,128]{1,0:T(8,128)S(1)}, u32[]{:S(2)}, u32[]{:S(2)}) %collective-permute-start) | collective-permute-done | bytes 4128 | tf_op jit(solution)/shard_map/ppermute | solution.py:324
  37.4 0.7 shard_map.86
  38.1 4.5 %all-to-all-start.1 = ((f32[32,16,128]{2,1,0:T(8,128)}), f32[32,16,128]{2,1,0:T(8,128)S(1)}, u32[]{:S(2)}, u32[]{:S(2)}) async-start(f32[32,16,128]{2,1,0:T(8,128)} %bitcast.34), calls=%async_computation.1 | async-start | bytes 524288 | tf_op jit(solution)/shard_map/all_to_all | solution.py:299
  42.6 1.9 %collective-permute-start.1 = (f32[320,256]{1,0:T(8,128)S(1)}, f32[320,256]{1,0:T(8,128)S(1)}, u32[]{:S(2)}, u32[]{:S(2)}) collective-permute-start(f32[320,256]{1,0:T(8,128)S(1)} %get-tuple-element.22), channel_id=1, source_target_pairs={{32,0},{33,1},{34,2},{35,3},{36,4},{37,5},{38,6},{39,7},{40,8},{41... | collective-permute-start | bytes 983048 | tf_op jit(solution)/shard_map/ppermute | solution.py:321
  44.5 12.3 %collective-permute-done.1.rim = f32[320,256]{1,0:T(8,128)S(1)} collective-permute-done((f32[320,256]{1,0:T(8,128)S(1)}, f32[320,256]{1,0:T(8,128)S(1)}, u32[]{:S(2)}, u32[]{:S(2)}) %collective-permute-start.1) | collective-permute-done | bytes 327712 | tf_op jit(solution)/shard_map/ppermute | solution.py:321
  56.8 3.1 %band.1 = (bf16[3,256,256]{2,1,0:T(8,128)(2,1)S(1)}, bf16[3,256,256]{2,1,0:T(8,128)(2,1)S(1)}, bf16[3,256,256]{2,1,0:T(8,128)(2,1)S(1)}, bf16[3,256,256]{2,1,0:T...) custom-call(s32[1]{0:T(128)} %bitcast.place.refs_0_, f32[320,256]{1,0:T(8,128)S(1)} %collective-permute-done.1.rim, ...), custom_call_target="tpu_custom_call" | custom-call | tf_op jit(solution)/shard_map/band/pallas_call | solution.py:258
  60.0 1.9 %collective-permute-start.2 = (f32[64,640]{1,0:T(8,128)S(1)}, f32[64,640]{1,0:T(8,128)S(1)}, u32[]{:S(2)}, u32[]{:S(2)}) collective-permute-start(f32[64,640]{1,0:T(8,128)S(1)} %get-tuple-element.28), channel_id=1, source_target_pairs={{0,32},{32,0},{64,96},{96,64},{128,160},{160,128},{192,224},{224,1... | collective-permute-start | bytes 491528 | tf_op jit(solution)/shard_map/ppermute | solution.py:328
  61.9 1.4 %collective-permute-done.2.got = f32[64,640]{1,0:T(8,128)S(1)} collective-permute-done((f32[64,640]{1,0:T(8,128)S(1)}, f32[64,640]{1,0:T(8,128)S(1)}, u32[]{:S(2)}, u32[]{:S(2)}) %collective-permute-start.2) | collective-permute-done | bytes 163872 | tf_op jit(solution)/shard_map/ppermute | solution.py:328
  63.2 0.0 all-to-all-done.1
  63.2 0.0 copy-start
  63.3 3.1 %whiten_and_project.1 = (f32[64,2048]{1,0:T(8,128)S(1)}, f32[64,512]{1,0:T(8,128)S(1)}) custom-call(s32[1]{0:T(128)} %bitcast.place.refs_0_, f32[512,128]{1,0:T(8,128)S(1)} %bitcast.28, bf16[3,256,256]{2,1,0:T(8,128)(2,1)S(1)} %get-tuple-element.23.b0, bf16[3,256,256]{2,1,0:T(8,128)(2,1)S(1)} %get-tuple-element.24.b1, ...), custom_call_target="tpu_custom_call" | custom-call | tf_op jit(solution)/shard_map/whiten_and_project/pallas_call | solution.py:287
  66.4 0.0 copy-start.1
  66.4 0.0 copy-start.2
  66.4 13.8 %all_to_all.55 = f32[8,8,2048]{2,1,0:T(8,128)S(1)} all-to-all(f32[8,8,2048]{2,1,0:T(8,128)S(1)} %bitcast.30), channel_id=1, replica_groups={{0,32,128,160,256,288,384,416},{64,96,192,224,320,352,448,480},{1,33,12..., dimensions={0} | all-to-all | bytes 1048576 | tf_op jit(solution)/shard_map/all_to_all | solution.py:299
  80.2 4.9 %collective-permute-start.3 = (f32[8,2688]{1,0:T(8,128)S(1)}, f32[8,2688]{1,0:T(8,128)S(1)}, u32[]{:S(2)}, u32[]{:S(2)}) collective-permute-start(f32[8,2688]{1,0:T(8,128)S(1)} %shard_map.87.refs_1_), channel_id=1, source_target_pairs={{0,64},{32,96},{64,0},{96,32},{128,192},{160,224},{192,128},{224,1... | collective-permute-start | bytes 258056 | tf_op jit(solution)/shard_map/ppermute | solution.py:331
  85.1 4.3 %collective-permute-done.3.refs_2_ = f32[8,2688]{1,0:T(8,128)S(1)} collective-permute-done((f32[8,2688]{1,0:T(8,128)S(1)}, f32[8,2688]{1,0:T(8,128)S(1)}, u32[]{:S(2)}, u32[]{:S(2)}) %collective-permute-start.3) | collective-permute-done | bytes 86048 | tf_op jit(solution)/shard_map/ppermute | solution.py:331
  89.4 0.8 shard_map.88
  90.2 19.6 %all_to_all.56 = f32[32,1,128]{2,1,0:T(1,128)S(1)} all-to-all(f32[32,1,128]{2,1,0:T(1,128)} %bitcast.37), channel_id=1, replica_groups=mesh['tm'=16,'coef'=32] {'coef'}, dimensions={0} | all-to-all | bytes 32768 | tf_op jit(solution)/shard_map/all_to_all | solution.py:299
  109.8 0.0 copy-done
  109.8 0.8 shard_map.90
  110.6 5.7 %all-to-all-start.4 = ((f32[8,8,1280]{2,1,0:T(8,128)}), f32[8,8,1280]{2,1,0:T(8,128)S(1)}, u32[]{:S(2)}, u32[]{:S(2)}) async-start(f32[8,8,1280]{2,1,0:T(8,128)} %bitcast.16), calls=%async_computation.4 | async-start | bytes 655360 | tf_op jit(solution)/shard_map/all_to_all | solution.py:299
  116.4 0.0 copy-done.1
  116.4 0.0 copy-done.2
  116.4 0.9 shard_map.89
  117.3 6.2 %all-to-all-done.4 = f32[8,8,1280]{2,1,0:T(8,128)S(1)} async-done(((f32[8,8,1280]{2,1,0:T(8,128)}), f32[8,8,1280]{2,1,0:T(8,128)S(1)}, u32[]{:S(2)}, u32[]{:S(2)}) %all-to-all-start.4) | async-done | bytes 327712 | tf_op jit(solution)/shard_map/all_to_all | solution.py:299
  123.5 0.7 copy.12
  (2 shorter events, 0.1 us)
Async XLA Ops:
  28.1 9.2 %collective-permute-start = (f32[8,128]{1,0:T(8,128)S(1)}, f32[8,128]{1,0:T(8,128)S(1)}, u32[]{:S(2)}, u32[]{:S(2)}) collective-permute-start(f32[8,128]{1,0:T(8,128)S(1)} %get-tuple-element.21.refs_0_), channel_id=1, source_target_pairs={{16,48},{17,49},{18,50},{19,51},{20,52},{21,53},{22,54},{23,55},{2... | collective-permute-start | bytes 12296 | tf_op jit(solution)/shard_map/ppermute | solution.py:324
  38.1 25.2 %all-to-all-start.1 = ((f32[32,16,128]{2,1,0:T(8,128)}), f32[32,16,128]{2,1,0:T(8,128)S(1)}, u32[]{:S(2)}, u32[]{:S(2)}) async-start(f32[32,16,128]{2,1,0:T(8,128)} %bitcast.34), calls=%async_computation.1 | async-start | bytes 524288 | tf_op jit(solution)/shard_map/all_to_all | solution.py:299
  42.6 14.2 %collective-permute-start.1 = (f32[320,256]{1,0:T(8,128)S(1)}, f32[320,256]{1,0:T(8,128)S(1)}, u32[]{:S(2)}, u32[]{:S(2)}) collective-permute-start(f32[320,256]{1,0:T(8,128)S(1)} %get-tuple-element.22), channel_id=1, source_target_pairs={{32,0},{33,1},{34,2},{35,3},{36,4},{37,5},{38,6},{39,7},{40,8},{41... | collective-permute-start | bytes 983048 | tf_op jit(solution)/shard_map/ppermute | solution.py:321
  60.0 3.3 %collective-permute-start.2 = (f32[64,640]{1,0:T(8,128)S(1)}, f32[64,640]{1,0:T(8,128)S(1)}, u32[]{:S(2)}, u32[]{:S(2)}) collective-permute-start(f32[64,640]{1,0:T(8,128)S(1)} %get-tuple-element.28), channel_id=1, source_target_pairs={{0,32},{32,0},{64,96},{96,64},{128,160},{160,128},{192,224},{224,1... | collective-permute-start | bytes 491528 | tf_op jit(solution)/shard_map/ppermute | solution.py:328
  63.2 46.6 %copy-start = (f32[1280,64]{0,1:T(8,128)S(1)}, f32[1280,64]{0,1:T(8,128)}, u32[]{:S(2)}) copy-start(f32[1280,64]{0,1:T(8,128)} %param.9) | copy-start | bytes 983044
  66.4 50.0 %copy-start.1 = (f32[512,64]{0,1:T(8,128)S(1)}, f32[512,64]{0,1:T(8,128)}, u32[]{:S(2)}) copy-start(f32[512,64]{0,1:T(8,128)} %param.11) | copy-start | bytes 393220
  66.4 50.0 %copy-start.2 = (f32[1280,64]{0,1:T(8,128)S(1)}, f32[1280,64]{0,1:T(8,128)}, u32[]{:S(2)}) copy-start(f32[1280,64]{0,1:T(8,128)} %param.8) | copy-start | bytes 983044
  80.2 9.2 %collective-permute-start.3 = (f32[8,2688]{1,0:T(8,128)S(1)}, f32[8,2688]{1,0:T(8,128)S(1)}, u32[]{:S(2)}, u32[]{:S(2)}) collective-permute-start(f32[8,2688]{1,0:T(8,128)S(1)} %shard_map.87.refs_1_), channel_id=1, source_target_pairs={{0,64},{32,96},{64,0},{96,32},{128,192},{160,224},{192,128},{224,1... | collective-permute-start | bytes 258056 | tf_op jit(solution)/shard_map/ppermute | solution.py:331
  110.6 12.8 %all-to-all-start.4 = ((f32[8,8,1280]{2,1,0:T(8,128)}), f32[8,8,1280]{2,1,0:T(8,128)S(1)}, u32[]{:S(2)}, u32[]{:S(2)}) async-start(f32[8,8,1280]{2,1,0:T(8,128)} %bitcast.16), calls=%async_computation.4 | async-start | bytes 655360 | tf_op jit(solution)/shard_map/all_to_all | solution.py:299

commit v3 on v2

--- a/solution.py
+++ b/solution.py
@@ -22,6 +22,10 @@
     count = left.shape[0]
     first = lax.dot_general(jnp.concatenate([high, low], axis=0), right[0], dims, preferred_element_type=F32)
     return first[:count] + first[count:] + lax.dot_general(high, right[1], dims, preferred_element_type=F32)
+
+
+def joined(first, second, axis):
+    return tuple(jnp.concatenate([a, b], axis=axis) for a, b in zip(first, second, strict=True))
 
 
 def skew(rows):
@@ -75,7 +79,9 @@
         same.append(split(jnp.where(lane <= lag, full, 0.0)))
         before.append(split(jnp.where(lane > lag, full, 0.0)))
     res = [residual[:, :BLOCK], residual[:, BLOCK:], rim[BLOCK:]]
-    back = [times(res[b], same[b], NN) + times(res[b + 1], before[b + 1], NN) for b in range(2)]
+    back = [
+        times(jnp.concatenate(res[b : b + 2], axis=1), joined(same[b], before[b + 1], 0), NN) for b in range(2)
+    ]
     bands = [jnp.stack([m[k] for m in kind]) for kind in (same, before) for k in range(2)]
     return *bands, times(jnp.concatenate(back, axis=1), split(design()), NN)
 
@@ -98,10 +104,14 @@
         block((2, 3), 0),
         jnp.where(odd, block((0, 1), 8, 2), block((0, 1), 8)),
     ]
-    pred = [times(plain[b + 1], same[b], NT) + times(plain[b], before[b], NT) for b in range(3)]
+    pred = [
+        times(jnp.concatenate(plain[b : b + 2], axis=1), joined(before[b], same[b], 1), NT) for b in range(3)
+    ]
     own = jnp.concatenate(pred[:2], axis=1)
     energy = jnp.broadcast_to(row_squares(own), (64, 128))
-    spread = [times(pred[b], same[b], NN) + times(pred[b + 1], before[b + 1], NN) for b in range(2)]
+    spread = [
+        times(jnp.concatenate(pred[b : b + 2], axis=1), joined(same[b], before[b + 1], 0), NN) for b in range(2)
+    ]
     left = jnp.concatenate(spread, axis=1)
     parts = []
     for k in range(2 * keep.shape[1] // BLOCK):
@@ -198,8 +208,6 @@
         copy(gradient_prev, old_v, 1)
         for i in range(4):
             copy(design.at[128 * i : 128 * i + 128], des_v.at[128 * i : 128 * i + 128], 2 + i)
-        copy(whitening.at[:BLOCK], rim.at[:BLOCK], 6)
-        copy(residual.at[:, :BLOCK], rim.at[BLOCK:], 7)
         copies[0].wait()
         left = dir_v[...]
         copies[1].wait()
@@ -208,13 +216,20 @@
             rows_v[9 * m + 8 : 9 * m + 9] = old
         for i in range(4):
             copies[2 + i].wait()
+            if i == 2:
+                rims = [
+                    pltpu.make_async_copy(whitening.at[:BLOCK], rim.at[:BLOCK], sems.at[6]),
+                    pltpu.make_async_copy(residual.at[:, :BLOCK], rim.at[BLOCK:], sems.at[7]),
+                ]
+                for rows_out in rims:
+                    rows_out.start()
             part = times(left, split(des_v[128 * i : 128 * i + 128]), NT)
             for j in range(8):
                 first = 9 * (8 * i + j)
                 rows_v[first : first + 8] = part[8 * j : 8 * j + 8]
             copy(rows_v.at[72 * i : 72 * i + 72], rows.at[72 * i : 72 * i + 72], 8 + i)
-        for k in range(6, 12):
-            copies[k].wait()
+        for rows_out in rims + copies[6:]:
+            rows_out.wait()
 
     return pl.pallas_call(
         kernel,

time: 125 us -> 125 us (level)
  no operation moved by 1% of the time
where the time goes in v3:
time: 125 us; the launch traced here: 124 us
  blocking collectives  56.9 us (46%)
  waiting for transfers between devices  29.3 us (23%)
  starting transfers between devices  23.1 us (18%)
  Pallas kernels  13.3 us (11%)
    all_to_all x3, blocking collectives, exchange(): lax.all_to_all(rows, axis, 0, 0, axis_index_groups=groups, tiled=True)  56.9 us
    ppermute x1, waiting for transfers between devices, per_device(): lax.ppermute(rim, ('tm', 'coef'), neighbours(blocks_t, blocks_c, lambda c...  12.3 us
    all_to_all x2, starting transfers between devices, exchange(): lax.all_to_all(rows, axis, 0, 0, axis_index_groups=groups, tiled=True)  10.2 us
    all_to_all x2, waiting for transfers between devices, exchange(): lax.all_to_all(rows, axis, 0, 0, axis_index_groups=groups, tiled=True)  6.22 us
    ppermute x1, waiting for transfers between devices, per_device(): lax.ppermute(tile, ('tm', 'coef'), neighbours(blocks_t, blocks_c, lambda...  5.04 us
    ppermute x1, starting transfers between devices, per_device(): other = lax.ppermute(mine, 'tm', [(i, i ^ 2) for i in range(blocks_t)])  4.89 us
    ppermute x1, waiting for transfers between devices, per_device(): other = lax.ppermute(mine, 'tm', [(i, i ^ 2) for i in range(blocks_t)])  4.34 us
    ppermute x1, starting transfers between devices, per_device(): lax.ppermute(tile, ('tm', 'coef'), neighbours(blocks_t, blocks_c, lambda...  4.18 us
  transfers between devices with their start and end apart: 6, of which 5 were waited for; matrix products, arithmetic and copies ran while one was open for 0% of the time, Pallas kernels for 3%

profile of v3, /device:TPU:1, one launch (start us, length us, event | category | flops | bytes accessed | tf_op | source)
XLA Modules:
  0.0 124.0 jit_solution(5413007343194801976)
XLA Ops:
  0.6 3.9 %predict.1 = (f32[288,128]{1,0:T(8,128)}, f32[320,256]{1,0:T(8,128)S(1)}) custom-call(f32[64,1280]{1,0:T(8,128)} %bitcast.21, f32[512,1280]{1,0:T(8,128)} %design.5, f32[64,1280]{1,0:T(8,128)} %bitcast.35, f32[512,256]{1,0:T(8,128)} %whitening.3, f32[64,512]{1,0:T(8,128)} %bitcast.25), custom_call_target="tpu_custom_call" | custom-call | tf_op jit(solution)/shard_map/predict/pallas_call | solution.py:234
  4.6 23.5 %all_to_all.54 = f32[32,1,1152]{2,1,0:T(1,128)S(1)} all-to-all(f32[32,1,1152]{2,1,0:T(1,128)} %bitcast.36), channel_id=1, replica_groups=mesh['tm'=16,'coef'=32] {'coef'}, dimensions={0} | all-to-all | bytes 294912 | tf_op jit(solution)/shard_map/all_to_all | solution.py:314
  28.1 4.2 %collective-permute-start = (f32[8,128]{1,0:T(8,128)S(1)}, f32[8,128]{1,0:T(8,128)S(1)}, u32[]{:S(2)}, u32[]{:S(2)}) collective-permute-start(f32[8,128]{1,0:T(8,128)S(1)} %get-tuple-element.21.refs_0_), channel_id=1, source_target_pairs={{16,48},{17,49},{18,50},{19,51},{20,52},{21,53},{22,54},{23,55},{2... | collective-permute-start | bytes 12296 | tf_op jit(solution)/shard_map/ppermute | solution.py:339
  32.3 5.0 %collective-permute-done.refs_1_ = f32[8,128]{1,0:T(8,128)S(1)} collective-permute-done((f32[8,128]{1,0:T(8,128)S(1)}, f32[8,128]{1,0:T(8,128)S(1)}, u32[]{:S(2)}, u32[]{:S(2)}) %collective-permute-start) | collective-permute-done | bytes 4128 | tf_op jit(solution)/shard_map/ppermute | solution.py:339
  37.4 0.7 shard_map.86
  38.1 4.5 %all-to-all-start.1 = ((f32[32,16,128]{2,1,0:T(8,128)}), f32[32,16,128]{2,1,0:T(8,128)S(1)}, u32[]{:S(2)}, u32[]{:S(2)}) async-start(f32[32,16,128]{2,1,0:T(8,128)} %bitcast.34), calls=%async_computation.1 | async-start | bytes 524288 | tf_op jit(solution)/shard_map/all_to_all | solution.py:314
  42.6 1.9 %collective-permute-start.1 = (f32[320,256]{1,0:T(8,128)S(1)}, f32[320,256]{1,0:T(8,128)S(1)}, u32[]{:S(2)}, u32[]{:S(2)}) collective-permute-start(f32[320,256]{1,0:T(8,128)S(1)} %get-tuple-element.22), channel_id=1, source_target_pairs={{32,0},{33,1},{34,2},{35,3},{36,4},{37,5},{38,6},{39,7},{40,8},{41... | collective-permute-start | bytes 983048 | tf_op jit(solution)/shard_map/ppermute | solution.py:336
  44.5 12.3 %collective-permute-done.1.rim = f32[320,256]{1,0:T(8,128)S(1)} collective-permute-done((f32[320,256]{1,0:T(8,128)S(1)}, f32[320,256]{1,0:T(8,128)S(1)}, u32[]{:S(2)}, u32[]{:S(2)}) %collective-permute-start.1) | collective-permute-done | bytes 327712 | tf_op jit(solution)/shard_map/ppermute | solution.py:336
  56.8 3.1 %band.1 = (bf16[3,256,256]{2,1,0:T(8,128)(2,1)S(1)}, bf16[3,256,256]{2,1,0:T(8,128)(2,1)S(1)}, bf16[3,256,256]{2,1,0:T(8,128)(2,1)S(1)}, bf16[3,256,256]{2,1,0:T...) custom-call(s32[1]{0:T(128)} %bitcast.place.refs_0_, f32[320,256]{1,0:T(8,128)S(1)} %collective-permute-done.1.rim, ...), custom_call_target="tpu_custom_call" | custom-call | tf_op jit(solution)/shard_map/band/pallas_call | solution.py:273
  59.9 1.9 %collective-permute-start.2 = (f32[64,640]{1,0:T(8,128)S(1)}, f32[64,640]{1,0:T(8,128)S(1)}, u32[]{:S(2)}, u32[]{:S(2)}) collective-permute-start(f32[64,640]{1,0:T(8,128)S(1)} %get-tuple-element.28), channel_id=1, source_target_pairs={{0,32},{32,0},{64,96},{96,64},{128,160},{160,128},{192,224},{224,1... | collective-permute-start | bytes 491528 | tf_op jit(solution)/shard_map/ppermute | solution.py:343
  61.9 1.4 %collective-permute-done.2.got = f32[64,640]{1,0:T(8,128)S(1)} collective-permute-done((f32[64,640]{1,0:T(8,128)S(1)}, f32[64,640]{1,0:T(8,128)S(1)}, u32[]{:S(2)}, u32[]{:S(2)}) %collective-permute-start.2) | collective-permute-done | bytes 163872 | tf_op jit(solution)/shard_map/ppermute | solution.py:343
  63.2 0.0 all-to-all-done.1
  63.2 0.0 copy-start
  63.2 2.9 %whiten_and_project.1 = (f32[64,2048]{1,0:T(8,128)S(1)}, f32[64,512]{1,0:T(8,128)S(1)}) custom-call(s32[1]{0:T(128)} %bitcast.place.refs_0_, f32[512,128]{1,0:T(8,128)S(1)} %bitcast.28, bf16[3,256,256]{2,1,0:T(8,128)(2,1)S(1)} %get-tuple-element.23.b0, bf16[3,256,256]{2,1,0:T(8,128)(2,1)S(1)} %get-tuple-element.24.b1, ...), custom_call_target="tpu_custom_call" | custom-call | tf_op jit(solution)/shard_map/whiten_and_project/pallas_call | solution.py:302
  66.2 0.0 copy-start.1
  66.2 0.0 copy-start.2
  66.2 13.8 %all_to_all.55 = f32[8,8,2048]{2,1,0:T(8,128)S(1)} all-to-all(f32[8,8,2048]{2,1,0:T(8,128)S(1)} %bitcast.30), channel_id=1, replica_groups={{0,32,128,160,256,288,384,416},{64,96,192,224,320,352,448,480},{1,33,12..., dimensions={0} | all-to-all | bytes 1048576 | tf_op jit(solution)/shard_map/all_to_all | solution.py:314
  80.0 4.9 %collective-permute-start.3 = (f32[8,2688]{1,0:T(8,128)S(1)}, f32[8,2688]{1,0:T(8,128)S(1)}, u32[]{:S(2)}, u32[]{:S(2)}) collective-permute-start(f32[8,2688]{1,0:T(8,128)S(1)} %shard_map.87.refs_1_), channel_id=1, source_target_pairs={{0,64},{32,96},{64,0},{96,32},{128,192},{160,224},{192,128},{224,1... | collective-permute-start | bytes 258056 | tf_op jit(solution)/shard_map/ppermute | solution.py:346
  84.9 4.3 %collective-permute-done.3.refs_2_ = f32[8,2688]{1,0:T(8,128)S(1)} collective-permute-done((f32[8,2688]{1,0:T(8,128)S(1)}, f32[8,2688]{1,0:T(8,128)S(1)}, u32[]{:S(2)}, u32[]{:S(2)}) %collective-permute-start.3) | collective-permute-done | bytes 86048 | tf_op jit(solution)/shard_map/ppermute | solution.py:346
  89.2 0.8 shard_map.88
  90.0 19.6 %all_to_all.56 = f32[32,1,128]{2,1,0:T(1,128)S(1)} all-to-all(f32[32,1,128]{2,1,0:T(1,128)} %bitcast.37), channel_id=1, replica_groups=mesh['tm'=16,'coef'=32] {'coef'}, dimensions={0} | all-to-all | bytes 32768 | tf_op jit(solution)/shard_map/all_to_all | solution.py:314
  109.6 0.0 copy-done
  109.6 0.8 shard_map.90
  110.4 5.7 %all-to-all-start.4 = ((f32[8,8,1280]{2,1,0:T(8,128)}), f32[8,8,1280]{2,1,0:T(8,128)S(1)}, u32[]{:S(2)}, u32[]{:S(2)}) async-start(f32[8,8,1280]{2,1,0:T(8,128)} %bitcast.16), calls=%async_computation.4 | async-start | bytes 655360 | tf_op jit(solution)/shard_map/all_to_all | solution.py:314
  116.2 0.0 copy-done.1
  116.2 0.0 copy-done.2
  116.2 0.9 shard_map.89
  117.1 6.2 %all-to-all-done.4 = f32[8,8,1280]{2,1,0:T(8,128)S(1)} async-done(((f32[8,8,1280]{2,1,0:T(8,128)}), f32[8,8,1280]{2,1,0:T(8,128)S(1)}, u32[]{:S(2)}, u32[]{:S(2)}) %all-to-all-start.4) | async-done | bytes 327712 | tf_op jit(solution)/shard_map/all_to_all | solution.py:314
  123.3 0.7 copy.12
  (2 shorter events, 0.1 us)
Async XLA Ops:
  28.1 9.2 %collective-permute-start = (f32[8,128]{1,0:T(8,128)S(1)}, f32[8,128]{1,0:T(8,128)S(1)}, u32[]{:S(2)}, u32[]{:S(2)}) collective-permute-start(f32[8,128]{1,0:T(8,128)S(1)} %get-tuple-element.21.refs_0_), channel_id=1, source_target_pairs={{16,48},{17,49},{18,50},{19,51},{20,52},{21,53},{22,54},{23,55},{2... | collective-permute-start | bytes 12296 | tf_op jit(solution)/shard_map/ppermute | solution.py:339
  38.1 25.2 %all-to-all-start.1 = ((f32[32,16,128]{2,1,0:T(8,128)}), f32[32,16,128]{2,1,0:T(8,128)S(1)}, u32[]{:S(2)}, u32[]{:S(2)}) async-start(f32[32,16,128]{2,1,0:T(8,128)} %bitcast.34), calls=%async_computation.1 | async-start | bytes 524288 | tf_op jit(solution)/shard_map/all_to_all | solution.py:314
  42.6 14.2 %collective-permute-start.1 = (f32[320,256]{1,0:T(8,128)S(1)}, f32[320,256]{1,0:T(8,128)S(1)}, u32[]{:S(2)}, u32[]{:S(2)}) collective-permute-start(f32[320,256]{1,0:T(8,128)S(1)} %get-tuple-element.22), channel_id=1, source_target_pairs={{32,0},{33,1},{34,2},{35,3},{36,4},{37,5},{38,6},{39,7},{40,8},{41... | collective-permute-start | bytes 983048 | tf_op jit(solution)/shard_map/ppermute | solution.py:336
  59.9 3.3 %collective-permute-start.2 = (f32[64,640]{1,0:T(8,128)S(1)}, f32[64,640]{1,0:T(8,128)S(1)}, u32[]{:S(2)}, u32[]{:S(2)}) collective-permute-start(f32[64,640]{1,0:T(8,128)S(1)} %get-tuple-element.28), channel_id=1, source_target_pairs={{0,32},{32,0},{64,96},{96,64},{128,160},{160,128},{192,224},{224,1... | collective-permute-start | bytes 491528 | tf_op jit(solution)/shard_map/ppermute | solution.py:343
  63.2 46.4 %copy-start = (f32[1280,64]{0,1:T(8,128)S(1)}, f32[1280,64]{0,1:T(8,128)}, u32[]{:S(2)}) copy-start(f32[1280,64]{0,1:T(8,128)} %param.9) | copy-start | bytes 983044
  66.2 50.0 %copy-start.1 = (f32[512,64]{0,1:T(8,128)S(1)}, f32[512,64]{0,1:T(8,128)}, u32[]{:S(2)}) copy-start(f32[512,64]{0,1:T(8,128)} %param.11) | copy-start | bytes 393220
  66.2 50.0 %copy-start.2 = (f32[1280,64]{0,1:T(8,128)S(1)}, f32[1280,64]{0,1:T(8,128)}, u32[]{:S(2)}) copy-start(f32[1280,64]{0,1:T(8,128)} %param.8) | copy-start | bytes 983044
  80.0 9.2 %collective-permute-start.3 = (f32[8,2688]{1,0:T(8,128)S(1)}, f32[8,2688]{1,0:T(8,128)S(1)}, u32[]{:S(2)}, u32[]{:S(2)}) collective-permute-start(f32[8,2688]{1,0:T(8,128)S(1)} %shard_map.87.refs_1_), channel_id=1, source_target_pairs={{0,64},{32,96},{64,0},{96,32},{128,192},{160,224},{192,128},{224,1... | collective-permute-start | bytes 258056 | tf_op jit(solution)/shard_map/ppermute | solution.py:346
  110.4 12.8 %all-to-all-start.4 = ((f32[8,8,1280]{2,1,0:T(8,128)}), f32[8,8,1280]{2,1,0:T(8,128)S(1)}, u32[]{:S(2)}, u32[]{:S(2)}) async-start(f32[8,8,1280]{2,1,0:T(8,128)} %bitcast.16), calls=%async_computation.4 | async-start | bytes 655360 | tf_op jit(solution)/shard_map/all_to_all | solution.py:314
